TPU v7x, 256 devices: a whole 4x4x8 slice. The times are simulated.
256 devices in a mesh: dp: 16 (over z, core), mp: 16 (over y, x).
Axes of the slice: x: 4, y: 4, z: 8, core: 2. Of those that a mesh axis runs over, the one named last changes fastest.
Arguments:
- candidates: bfloat16 [4096, 4096], P('dp', 'mp'), may hold values from -6 to 6
- hold_gate: bfloat16 [4096, 8192], P(None, 'mp'), may hold values from -0.09375 to 0.09375
- hold_up: bfloat16 [4096, 8192], P(None, 'mp'), may hold values from -0.09375 to 0.09375
- probe: float32 [8192], P('mp'), as said below
- chosen: int32 [16, 192], replicated, may hold values from 0 to 4095, as said below
- counts: int32 [16], replicated, may hold values from 24 to 192, as said below
- gate_w: bfloat16 [4096, 14336], P('dp', 'mp'), may hold values from -0.09375 to 0.09375
- up_w: bfloat16 [4096, 14336], P('dp', 'mp'), may hold values from -0.09375 to 0.09375
- cotangent: bfloat16 [3072, 14336], P('dp', 'mp'), may hold values from -6 to 6
Outputs:
- grad_gate: bfloat16 [4096, 14336], P('dp', 'mp')
- grad_up: bfloat16 [4096, 14336], P('dp', 'mp')
- hidden: bfloat16 [3072, 14336], P('dp', 'mp')
- cand_weight: float32 [4096], P('dp')
Inputs may be any that keep to these rules, and one draw needn't show every extreme that they name: `chosen`: all entries are distinct candidate indices. `counts`: exactly one training shard uses all 192 slots in every draw. `probe`: magnitudes at most 12 / sqrt(8192).
All inputs are finite; a program needn't handle non-finite values.
Results may differ from a plain program's by a relative error of at most 0.0057.
Values may be sent and summed in bfloat16 or wider, within the bound.
A program may use at most 128 MiB of HBM per device.

v0:
```python
import jax
import jax.numpy as jnp
from jax import lax
from jax.sharding import PartitionSpec as P


def gather_by_a2a(x, axis_name, axis):
    parts = lax.psum(1, axis_name)
    stacked = lax.all_to_all(
        jnp.broadcast_to(x[None], (parts,) + x.shape),
        axis_name,
        split_axis=0,
        concat_axis=0,
        tiled=True,
    )
    stacked = jnp.moveaxis(stacked, 0, axis)
    shape = list(x.shape)
    shape[axis] *= parts
    return stacked.reshape(shape)


def gather_rows(x):
    by_z = lax.all_gather(x, "z", axis=0)
    both = lax.all_gather(by_z, "core", axis=1)
    return both.reshape((-1,) + x.shape[1:])


def on_device(candidates, hold_gate, hold_up, probe, chosen, counts, gate_w, up_w, cotangent):
    cand_dev = candidates.shape[0]
    shards = chosen.shape[0]
    slots = chosen.shape[1]
    full_w = (gather_rows(gate_w), gather_rows(up_w))
    own_index = lax.axis_index("z") * lax.psum(1, "core") + lax.axis_index("core")
    source = chosen // cand_dev
    local_row = (chosen % cand_dev).reshape(-1)
    usable = (
        (jnp.arange(slots, dtype=jnp.int32)[None, :] < counts[:, None]) & (source == own_index)
    ).reshape(-1)
    onehot = (
        (local_row[:, None] == jnp.arange(cand_dev, dtype=jnp.int32)[None, :]) & usable[:, None]
    ).astype(jnp.bfloat16)
    picked = jnp.dot(onehot, candidates, preferred_element_type=jnp.float32).astype(jnp.bfloat16)
    picked = picked.reshape(shards, slots, candidates.shape[1])
    arrived = lax.all_to_all(picked, DP, split_axis=0, concat_axis=0, tiled=True)
    row_slab = jnp.sum(arrived.astype(jnp.float32), axis=0).astype(jnp.bfloat16)
    row_x = gather_by_a2a(row_slab, "mp", 1)
    row_slices = lax.all_to_all(row_x, DP, split_axis=1, concat_axis=0, tiled=True)
    incoming = gather_by_a2a(candidates, "mp", 1)
    hold_g = jnp.dot(incoming, hold_gate, preferred_element_type=jnp.float32)
    hold_u = jnp.dot(incoming, hold_up, preferred_element_type=jnp.float32)
    partial_score = jnp.sum(jax.nn.silu(hold_g) * hold_u * probe[None, :], axis=1)
    score = lax.psum(partial_score, "mp")
    cand_weight = jax.nn.sigmoid(score)
    picked_weight = (
        jnp.dot(
            onehot, cand_weight.astype(jnp.bfloat16)[:, None], preferred_element_type=jnp.float32
        )
        .astype(jnp.bfloat16)
        .reshape(shards, slots)
    )
    arrived_weight = lax.all_to_all(picked_weight, DP, split_axis=0, concat_axis=0, tiled=True)
    row_weight = jnp.sum(arrived_weight.astype(jnp.float32), axis=0)
    gate = jnp.dot(row_x, full_w[0], preferred_element_type=jnp.float32)
    up = jnp.dot(row_x, full_w[1], preferred_element_type=jnp.float32)
    hidden = (jax.nn.silu(gate) * up).astype(jnp.bfloat16)
    back = cotangent.astype(jnp.float32) * row_weight[:, None]
    sig = jax.nn.sigmoid(gate)
    d_up = (back * gate * sig).astype(jnp.bfloat16)
    d_gate = (back * up * sig * (1.0 + gate * (1.0 - sig))).astype(jnp.bfloat16)
    contract_rows = (((0,), (0,)), ((), ()))
    incoming = (gather_rows(d_gate), gather_rows(d_up))
    grad_g = lax.dot_general(
        row_slices, incoming[0], contract_rows, preferred_element_type=jnp.float32
    )
    grad_u = lax.dot_general(
        row_slices, incoming[1], contract_rows, preferred_element_type=jnp.float32
    )
    return (grad_g.astype(jnp.bfloat16), grad_u.astype(jnp.bfloat16), hidden, cand_weight)


DP = ("z", "core")


def solution(mesh):
    cores = 2
    mesh = jax.sharding.Mesh(
        mesh.devices.reshape(mesh.devices.shape[0] // cores, cores, mesh.devices.shape[1]),
        ("z", "core", "mp"),
    )
    placed = (
        P(DP, "mp"),
        P(None, "mp"),
        P(None, "mp"),
        P("mp"),
        P(),
        P(),
        P(DP, "mp"),
        P(DP, "mp"),
        P(DP, "mp"),
    )
    return jax.shard_map(
        on_device,
        mesh=mesh,
        in_specs=placed,
        out_specs=(P(DP, "mp"), P(DP, "mp"), P(DP, "mp"), P(DP)),
        check_vma=False,
    )
```

profile of v0, /device:TPU:1, one launch (start us, length us, event | category | flops | bytes accessed | tf_op | source)
XLA Modules:
  0.0 406.3 jit_solution(17809317110289626407)
XLA Ops:
  8.7 54.6 %all-gather.21.cloned.1.call-done = bf16[2048,896]{1,0:T(8,128)(2,1)} async-done(((bf16[256,896]{1,0:T(8,128)(2,1)}), bf16[2048,896]{1,0:T(8,128)(2,1)}) %all-gather.21.cloned.1.call-update) | async-done | bytes 3670032 | tf_op jit(solution)/shard_map/all_gather | solution.py:23
  63.3 50.2 %all-gather.17.cloned.1.call-done = bf16[2048,896]{1,0:T(8,128)(2,1)} async-done(((bf16[256,896]{1,0:T(8,128)(2,1)}), bf16[2048,896]{1,0:T(8,128)(2,1)}) %all-gather.17.cloned.1.call-update) | async-done | bytes 3670032 | tf_op jit(solution)/shard_map/all_gather | solution.py:23
  113.7 1.5 broadcast_in_dim.5
  115.2 6.5 %all-to-all-start.3 = ((bf16[16,256,256]{1,2,0:T(8,128)(2,1)}), bf16[16,256,256]{1,2,0:T(8,128)(2,1)S(1)}, u32[]{:S(2)}, u32[]{:S(2)}) async-start(bf16[16,256,256]{1,2,0:T(8,128)(2,1)} %broadcast_in_dim.5), calls=%async_computation.3 | async-start | bytes 4194304 | tf_op jit(solution)/shard_map/all_to_all | solution.py:9
  122.0 3.5 convolution_convert_fusion
  125.5 26.5 %all-to-all-done.3 = bf16[16,256,256]{1,2,0:T(8,128)(2,1)S(1)} async-done(((bf16[16,256,256]{1,2,0:T(8,128)(2,1)}), bf16[16,256,256]{1,2,0:T(8,128)(2,1)S(1)}, u32[]{:S(2)}, u32[]{:S(2)}) %all-to-all-start.3) | async-done | bytes 2097184 | tf_op jit(solution)/shard_map/all_to_all | solution.py:9
  152.0 1.3 copy-done
  153.3 6.6 %all-to-all-start = ((bf16[16,192,256]{2,1,0:T(8,128)(2,1)}), bf16[16,192,256]{2,1,0:T(8,128)(2,1)S(1)}, u32[]{:S(2)}, u32[]{:S(2)}) async-start(bf16[16,192,256]{2,1,0:T(8,128)(2,1)} %bitcast.41), calls=%async_computation | async-start | bytes 3145728 | tf_op jit(solution)/shard_map/all_to_all | solution.py:44
  159.9 4.3 %fusion.15 = f32[256,512]{1,0:T(8,128)S(1)} fusion(bf16[256,4096]{0,1:T(8,128)(2,1)} %bitcast.39, bf16[4096,512]{1,0:T(8,128)(2,1)} %param.10), kind=kOutput, calls=%fused_computation.32 | convolution fusion | flops 1073741824 | bytes 6815744 | tf_op jit(solution)/shard_map/dot_general | solution.py:49
  164.6 1.4 fusion.9
  166.0 31.8 %psum.7 = f32[256]{0:T(256)S(1)} all-reduce(f32[256]{0:T(256)S(1)} %fusion.9), channel_id=1, replica_groups=mesh['z'=8,'core'=2,'mp'=16] {'mp'}, use_global_device_ids=true, to_apply=%region_2.3 | all-reduce | flops 256 | bytes 2048 | tf_op jit(solution)/shard_map/psum | solution.py:52
  198.4 2.5 fusion.1
  201.6 13.7 %all-to-all-start.4 = ((bf16[16,1,192]{2,1,0:T(2,128)(2,1)}), bf16[16,1,192]{2,1,0:T(2,128)(2,1)S(1)}, u32[]{:S(2)}, u32[]{:S(2)}) async-start(bf16[16,1,192]{2,1,0:T(2,128)(2,1)} %all_to_all.35), calls=%async_computation.4 | async-start | bytes 32768 | tf_op jit(solution)/shard_map/all_to_all | solution.py:61
  215.6 7.1 %all-to-all-done.4 = bf16[16,1,192]{2,1,0:T(2,128)(2,1)S(1)} async-done(((bf16[16,1,192]{2,1,0:T(2,128)(2,1)}), bf16[16,1,192]{2,1,0:T(2,128)(2,1)S(1)}, u32[]{:S(2)}, u32[]{:S(2)}) %all-to-all-start.4) | async-done | bytes 6176 | tf_op jit(solution)/shard_map/all_to_all | solution.py:61
  222.7 1.3 broadcast_in_dim.4
  224.0 3.7 all-to-all-start.1
  227.8 24.8 %all-to-all-done.1 = bf16[16,192,256]{2,1,0:T(8,128)(2,1)S(1)} async-done(((bf16[16,192,256]{2,1,0:T(8,128)(2,1)}), bf16[16,192,256]{2,1,0:T(8,128)(2,1)S(1)}, u32[]{:S(2)}, u32[]{:S(2)}) %all-to-all-start.1) | async-done | bytes 1572896 | tf_op jit(solution)/shard_map/all_to_all | solution.py:9
  252.9 5.8 %fusion.16 = f32[192,896]{1,0:T(8,128)} fusion(bf16[192,4096]{1,0:T(8,128)(2,1)S(1)} %bitcast.42, bf16[4096,896]{1,0:T(8,128)(2,1)} %bitcast.47), kind=kOutput, calls=%fused_computation.33 | convolution fusion | flops 1409286144 | bytes 9601024 | tf_op jit(solution)/shard_map/dot_general | solution.py:63
  258.7 6.1 %multiply_convert_fusion = (bf16[192,896]{1,0:T(8,128)(2,1)}, bf16[192,896]{1,0:T(8,128)(2,1)}, bf16[192,896]{1,0:T(8,128)(2,1)}) fusion(f32[192,896]{1,0:T(8,128)} %fusion.16, f32[192]{0:T(256)S(1)} %convert_reduce_fusion, bf16[192,896]{1,0:T(8,128)(2,1)S(1)} %copy-done.6, bf16[192,4096]{1,0:T(8,128)(2,1)S(1)} %bitcast.43, bf16[4096,896]{1,0:T(8,128)(2,1)} %bitcast.48), kind=kOutput, calls=%fused_computation.13 | convolution fusion | flops 1412382720 | bytes 10978048 | tf_op jit(solution)/shard_map/dot_general | solution.py:64
  265.5 32.7 %all-gather.29.cloned.1.call-done = bf16[1536,896]{1,0:T(8,128)(2,1)} async-done(((bf16[192,896]{1,0:T(8,128)(2,1)}), bf16[1536,896]{1,0:T(8,128)(2,1)}) %all-gather.29.cloned.1.call-update) | async-done | bytes 2752528 | tf_op jit(solution)/shard_map/all_gather | solution.py:23
  298.3 43.6 %all-gather.25.cloned.1.call-done = bf16[1536,896]{1,0:T(8,128)(2,1)} async-done(((bf16[192,896]{1,0:T(8,128)(2,1)}), bf16[1536,896]{1,0:T(8,128)(2,1)}) %all-gather.25.cloned.1.call-update) | async-done | bytes 2752528 | tf_op jit(solution)/shard_map/all_gather | solution.py:23
  341.9 47.2 %all_to_all.41 = bf16[192,16,256]{2,0,1:T(8,128)(2,1)S(1)} all-to-all(bf16[192,16,256]{2,0,1:T(8,128)(2,1)S(1)} %bitcast.34), channel_id=1, replica_groups=mesh['z'=8,'core'=2,'mp'=16] {'z','core'}, dimensions={1} | all-to-all | bytes 3145728 | tf_op jit(solution)/shard_map/all_to_all | solution.py:47
  389.1 5.2 %convolution_convert_fusion.1 = bf16[256,896]{1,0:T(8,128)(2,1)} fusion(bf16[3072,256]{1,0:T(8,128)(2,1)S(1)} %bitcast.44, bf16[3072,896]{1,0:T(8,128)(2,1)} %bitcast.49), kind=kOutput, calls=%fused_computation.8 | convolution fusion | flops 1409515520 | bytes 7536640 | tf_op jit(solution)/shard_map/dot_general | solution.py:75
  394.3 5.2 %convolution_convert_fusion.2 = bf16[256,896]{1,0:T(8,128)(2,1)} fusion(bf16[3072,256]{1,0:T(8,128)(2,1)S(1)} %bitcast.45, bf16[3072,896]{1,0:T(8,128)(2,1)} %bitcast.50), kind=kOutput, calls=%fused_computation.9 | convolution fusion | flops 1409515520 | bytes 7536640 | tf_op jit(solution)/shard_map/dot_general | solution.py:72
  (48 shorter events, 4.9 us)
Async XLA Ops:
  7.2 56.1 %all-gather.21.cloned.1.call-start = ((), (), s32[]{:S(2)}) async-start(), calls=%async_computation.7 | async-start | bytes 4128768 | tf_op jit(solution)/shard_map/all_gather | solution.py:23
  7.9 105.6 %all-gather.17.cloned.1.call-start = ((), (), s32[]{:S(2)}) async-start(), calls=%async_computation.5 | async-start | bytes 4128768 | tf_op jit(solution)/shard_map/all_gather | solution.py:23
  8.6 244.2 %all-gather.23.cloned.1.call-start = ((), (), s32[]{:S(2)}) async-start(), calls=%async_computation.8 | async-start | bytes 11010048 | tf_op jit(solution)/shard_map/all_gather | solution.py:24
  63.3 50.3 %copy-start.2 = (bf16[256,256]{1,0:T(8,128)(2,1)S(1)}, bf16[256,256]{1,0:T(8,128)(2,1)}, u32[]{:S(2)}) copy-start(bf16[256,256]{1,0:T(8,128)(2,1)} %param.9) | copy-start | bytes 393220
  63.3 195.5 %all-gather.19.cloned.1.call-start = ((), (), s32[]{:S(2)}) async-start(), calls=%async_computation.6 | async-start | bytes 11010048 | tf_op jit(solution)/shard_map/all_gather | solution.py:24
  113.6 8.1 %copy-start.3 = (s32[16,192]{1,0:T(8,128)S(1)}, s32[16,192]{1,0:T(8,128)}, u32[]{:S(2)}) copy-start(s32[16,192]{1,0:T(8,128)} %param.13) | copy-start | bytes 36868
  113.7 8.1 %copy-start.4 = (s32[16]{0:T(128)S(1)}, s32[16]{0:T(128)}, u32[]{:S(2)}) copy-start(s32[16]{0:T(128)} %param.14) | copy-start | bytes 196
  115.2 36.8 %all-to-all-start.3 = ((bf16[16,256,256]{1,2,0:T(8,128)(2,1)}), bf16[16,256,256]{1,2,0:T(8,128)(2,1)S(1)}, u32[]{:S(2)}, u32[]{:S(2)}) async-start(bf16[16,256,256]{1,2,0:T(8,128)(2,1)} %broadcast_in_dim.5), calls=%async_computation.3 | async-start | bytes 4194304 | tf_op jit(solution)/shard_map/all_to_all | solution.py:9
  152.0 1.3 copy-start
  153.3 48.3 %all-to-all-start = ((bf16[16,192,256]{2,1,0:T(8,128)(2,1)}), bf16[16,192,256]{2,1,0:T(8,128)(2,1)S(1)}, u32[]{:S(2)}, u32[]{:S(2)}) async-start(bf16[16,192,256]{2,1,0:T(8,128)(2,1)} %bitcast.41), calls=%async_computation | async-start | bytes 3145728 | tf_op jit(solution)/shard_map/all_to_all | solution.py:44
  159.9 4.3 %copy-start.1 = (bf16[16,256,256]{1,2,0:T(8,128)(2,1)S(1)}, bf16[16,256,256]{1,2,0:T(8,128)(2,1)}, u32[]{:S(2)}) copy-start(bf16[16,256,256]{1,2,0:T(8,128)(2,1)} %copy-done) | copy-start | bytes 6291460
  159.9 4.8 %copy-start.5 = (bf16[4096,512]{1,0:T(8,128)(2,1)S(1)}, bf16[4096,512]{1,0:T(8,128)(2,1)}, u32[]{:S(2)}) copy-start(bf16[4096,512]{1,0:T(8,128)(2,1)} %param.11) | copy-start | bytes 12582916
  159.9 4.8 %copy-start.7 = (f32[512]{0:T(512)S(1)}, f32[512]{0:T(512)}, u32[]{:S(2)}) copy-start(f32[512]{0:T(512)} %param.12) | copy-start | bytes 6148
  201.6 21.1 %all-to-all-start.4 = ((bf16[16,1,192]{2,1,0:T(2,128)(2,1)}), bf16[16,1,192]{2,1,0:T(2,128)(2,1)S(1)}, u32[]{:S(2)}, u32[]{:S(2)}) async-start(bf16[16,1,192]{2,1,0:T(2,128)(2,1)} %all_to_all.35), calls=%async_computation.4 | async-start | bytes 32768 | tf_op jit(solution)/shard_map/all_to_all | solution.py:61
  224.0 28.6 %all-to-all-start.1 = ((bf16[16,192,256]{2,1,0:T(8,128)(2,1)}), bf16[16,192,256]{2,1,0:T(8,128)(2,1)S(1)}, u32[]{:S(2)}, u32[]{:S(2)}) async-start(bf16[16,192,256]{2,1,0:T(8,128)(2,1)} %broadcast_in_dim.4), calls=%async_computation.1 | async-start | bytes 3145728 | tf_op jit(solution)/shard_map/all_to_all | solution.py:9
  227.8 70.5 %all-gather.29.cloned.1.call-start = ((), (), s32[]{:S(2)}) async-start(), calls=%async_computation.11 | async-start | bytes 3096576 | tf_op jit(solution)/shard_map/all_gather | solution.py:23
  252.9 5.9 %copy-start.6 = (bf16[192,896]{1,0:T(8,128)(2,1)S(1)}, bf16[192,896]{1,0:T(8,128)(2,1)}, u32[]{:S(2)}) copy-start(bf16[192,896]{1,0:T(8,128)(2,1)} %param.17) | copy-start | bytes 1032196
  264.9 77.0 %all-gather.25.cloned.1.call-start = ((), (), s32[]{:S(2)}) async-start(), calls=%async_computation.9 | async-start | bytes 3096576 | tf_op jit(solution)/shard_map/all_gather | solution.py:23
  265.5 123.6 %all-gather.31.cloned.1.call-start = ((), (), s32[]{:S(2)}) async-start(), calls=%async_computation.12 | async-start | bytes 8257536 | tf_op jit(solution)/shard_map/all_gather | solution.py:24
  298.3 96.0 %all-gather.27.cloned.1.call-start = ((), (), s32[]{:S(2)}) async-start(), calls=%async_computation.10 | async-start | bytes 8257536 | tf_op jit(solution)/shard_map/all_gather | solution.py:24
Sparse Core Ops, SparseCore 0:
  9.8 53.4 all-gather.20
  65.0 48.4 all-gather.16
  115.3 23.1 all-gather.22
  140.1 25.0 all-gather.18
  265.0 33.1 all-gather.28
  300.4 41.3 all-gather.24
  343.6 23.0 all-gather.30
  368.5 22.2 all-gather.26
where the time goes:
time: 407 us; the launch traced here: 406 us
  waiting for transfers between devices  241 us (59%)
  blocking collectives  79.1 us (19%)
  matrix products  33.9 us (8%)
  starting transfers between devices  30.9 us (8%)
  between operations  14.3 us (4%)
  local copies, waits for them, and re-layouts  5.83 us (1%)
    all_gather x4, waiting for transfers between devices, gather_rows(): by_z = lax.all_gather(x, 'z', axis=0)  181 us
    all_to_all x2, waiting for transfers between devices, gather_by_a2a(): lax.all_to_all(jnp.broadcast_to(x[None], (parts,) + x.shape), axis_name,...  51.3 us
    all_to_all x1, blocking collectives, on_device(): lax.all_to_all(row_x, DP, split_axis=1, concat_axis=0, tiled=True)  47.2 us
    psum x1, blocking collectives, on_device(): score = lax.psum(partial_score, 'mp')  31.8 us
    all_to_all x1, starting transfers between devices, on_device(): lax.all_to_all(picked_weight, DP, split_axis=0, concat_axis=0, tiled=True)  13.7 us
    all_to_all x2, starting transfers between devices, gather_by_a2a(): lax.all_to_all(jnp.broadcast_to(x[None], (parts,) + x.shape), axis_name,...  10.2 us
  transfers between devices with their start and end apart: 12, of which 7 were waited for; matrix products, arithmetic and copies ran while one was open for 7% of the time, Pallas kernels for 0%

commit v1 on v0

--- a/solution.py
+++ b/solution.py
@@ -44,7 +44,9 @@
     arrived = lax.all_to_all(picked, DP, split_axis=0, concat_axis=0, tiled=True)
     row_slab = jnp.sum(arrived.astype(jnp.float32), axis=0).astype(jnp.bfloat16)
     row_x = gather_by_a2a(row_slab, "mp", 1)
-    row_slices = lax.all_to_all(row_x, DP, split_axis=1, concat_axis=0, tiled=True)
+    row_slices = jnp.concatenate(
+        lax.all_to_all(jnp.stack(jnp.split(row_x, lax.axis_size(DP), axis=1)), DP, 0, 0), axis=0
+    )
     incoming = gather_by_a2a(candidates, "mp", 1)
     hold_g = jnp.dot(incoming, hold_gate, preferred_element_type=jnp.float32)
     hold_u = jnp.dot(incoming, hold_up, preferred_element_type=jnp.float32)

time: 407 us -> 407 us (level)
  transfers between devices with their start and end apart: 12 -> 12, of which waited for: 7 -> 7; matrix products, arithmetic and copies ran while one was open for 7% -> 6% of each run, Pallas kernels for 0% -> 0%
where the time goes in v1:
time: 407 us; the launch traced here: 406 us
  waiting for transfers between devices  241 us (59%)
  blocking collectives  78.7 us (19%)
  matrix products  32.8 us (8%)
  starting transfers between devices  31.1 us (8%)
  between operations  14.4 us (4%)
  local copies, waits for them, and re-layouts  6.86 us (2%)
    all_gather x4, waiting for transfers between devices, gather_rows(): by_z = lax.all_gather(x, 'z', axis=0)  181 us
    all_to_all x2, waiting for transfers between devices, gather_by_a2a(): lax.all_to_all(jnp.broadcast_to(x[None], (parts,) + x.shape), axis_name,...  51.3 us
    all_to_all x1, blocking collectives, on_device(): lax.all_to_all(jnp.stack(jnp.split(row_x, lax.axis_size(DP), axis=1)), DP...  47.2 us
    psum x1, blocking collectives, on_device(): score = lax.psum(partial_score, 'mp')  31.5 us
    all_to_all x1, starting transfers between devices, on_device(): lax.all_to_all(picked_weight, DP, split_axis=0, concat_axis=0, tiled=True)  13.8 us
    all_to_all x2, starting transfers between devices, gather_by_a2a(): lax.all_to_all(jnp.broadcast_to(x[None], (parts,) + x.shape), axis_name,...  10.4 us
  transfers between devices with their start and end apart: 12, of which 7 were waited for; matrix products, arithmetic and copies ran while one was open for 6% of the time, Pallas kernels for 0%

profile of v1, /device:TPU:1, one launch (start us, length us, event | category | flops | bytes accessed | tf_op | source)
XLA Modules:
  0.0 406.1 jit_solution(143910329578058968)
XLA Ops:
  8.7 54.6 %all-gather.21.cloned.1.call-done = bf16[2048,896]{1,0:T(8,128)(2,1)} async-done(((bf16[256,896]{1,0:T(8,128)(2,1)}), bf16[2048,896]{1,0:T(8,128)(2,1)}) %all-gather.21.cloned.1.call-update) | async-done | bytes 3670032 | tf_op jit(solution)/shard_map/all_gather | solution.py:23
  63.3 50.2 %all-gather.17.cloned.1.call-done = bf16[2048,896]{1,0:T(8,128)(2,1)} async-done(((bf16[256,896]{1,0:T(8,128)(2,1)}), bf16[2048,896]{1,0:T(8,128)(2,1)}) %all-gather.17.cloned.1.call-update) | async-done | bytes 3670032 | tf_op jit(solution)/shard_map/all_gather | solution.py:23
  114.5 1.5 broadcast_in_dim.5
  116.0 6.7 %all-to-all-start.3 = ((bf16[16,256,256]{1,2,0:T(8,128)(2,1)}), bf16[16,256,256]{1,2,0:T(8,128)(2,1)S(1)}, u32[]{:S(2)}, u32[]{:S(2)}) async-start(bf16[16,256,256]{1,2,0:T(8,128)(2,1)} %broadcast_in_dim.5), calls=%async_computation.3 | async-start | bytes 4194304 | tf_op jit(solution)/shard_map/all_to_all | solution.py:9
  123.0 3.5 convolution_convert_fusion
  126.5 26.5 %all-to-all-done.3 = bf16[16,256,256]{1,2,0:T(8,128)(2,1)S(1)} async-done(((bf16[16,256,256]{1,2,0:T(8,128)(2,1)}), bf16[16,256,256]{1,2,0:T(8,128)(2,1)S(1)}, u32[]{:S(2)}, u32[]{:S(2)}) %all-to-all-start.3) | async-done | bytes 2097184 | tf_op jit(solution)/shard_map/all_to_all | solution.py:9
  152.9 1.3 copy-done
  154.3 6.6 %all-to-all-start = ((bf16[16,192,256]{2,1,0:T(8,128)(2,1)}), bf16[16,192,256]{2,1,0:T(8,128)(2,1)S(1)}, u32[]{:S(2)}, u32[]{:S(2)}) async-start(bf16[16,192,256]{2,1,0:T(8,128)(2,1)} %bitcast.120), calls=%async_computation | async-start | bytes 3145728 | tf_op jit(solution)/shard_map/all_to_all | solution.py:44
  160.9 4.2 %fusion.31 = f32[256,512]{1,0:T(8,128)S(1)} fusion(bf16[256,4096]{0,1:T(8,128)(2,1)} %bitcast.118, bf16[4096,512]{1,0:T(8,128)(2,1)} %param.10), kind=kOutput, calls=%fused_computation.64 | convolution fusion | flops 1073741824 | bytes 6815744 | tf_op jit(solution)/shard_map/dot_general | solution.py:51
  165.5 1.4 fusion.9
  166.9 31.5 %psum.7 = f32[256]{0:T(256)S(1)} all-reduce(f32[256]{0:T(256)S(1)} %fusion.9), channel_id=1, replica_groups=mesh['z'=8,'core'=2,'mp'=16] {'mp'}, use_global_device_ids=true, to_apply=%region_2.3 | all-reduce | flops 256 | bytes 2048 | tf_op jit(solution)/shard_map/psum | solution.py:54
  199.0 2.5 fusion.1
  202.2 13.8 %all-to-all-start.4 = ((bf16[16,1,192]{2,1,0:T(2,128)(2,1)}), bf16[16,1,192]{2,1,0:T(2,128)(2,1)S(1)}, u32[]{:S(2)}, u32[]{:S(2)}) async-start(bf16[16,1,192]{2,1,0:T(2,128)(2,1)} %all_to_all.24), calls=%async_computation.4 | async-start | bytes 32768 | tf_op jit(solution)/shard_map/all_to_all | solution.py:63
  216.2 7.1 %all-to-all-done.4 = bf16[16,1,192]{2,1,0:T(2,128)(2,1)S(1)} async-done(((bf16[16,1,192]{2,1,0:T(2,128)(2,1)}), bf16[16,1,192]{2,1,0:T(2,128)(2,1)S(1)}, u32[]{:S(2)}, u32[]{:S(2)}) %all-to-all-start.4) | async-done | bytes 6176 | tf_op jit(solution)/shard_map/all_to_all | solution.py:63
  223.3 1.3 broadcast_in_dim.4
  224.7 3.7 all-to-all-start.1
  228.5 24.8 %all-to-all-done.1 = bf16[16,192,256]{2,1,0:T(8,128)(2,1)S(1)} async-done(((bf16[16,192,256]{2,1,0:T(8,128)(2,1)}), bf16[16,192,256]{2,1,0:T(8,128)(2,1)S(1)}, u32[]{:S(2)}, u32[]{:S(2)}) %all-to-all-start.1) | async-done | bytes 1572896 | tf_op jit(solution)/shard_map/all_to_all | solution.py:9
  253.5 4.9 %fusion.32 = f32[192,896]{1,0:T(8,128)S(1)} fusion(bf16[192,4096]{1,0:T(8,128)(2,1)S(1)} %bitcast.96, bf16[4096,896]{1,0:T(8,128)(2,1)} %bitcast.124), kind=kOutput, calls=%fused_computation.65 | convolution fusion | flops 1409286144 | bytes 9601024 | tf_op jit(solution)/shard_map/dot_general | solution.py:65
  258.5 6.0 %multiply_convert_fusion = (bf16[192,896]{1,0:T(8,128)(2,1)}, bf16[192,896]{1,0:T(8,128)(2,1)}, bf16[192,896]{1,0:T(8,128)(2,1)}) fusion(f32[192,896]{1,0:T(8,128)S(1)} %fusion.32, f32[192]{0:T(256)S(1)} %convert_reduce_fusion, bf16[192,896]{1,0:T(8,128)(2,1)S(1)} %copy-done.6, bf16[192,4096]{1,0:T(8,128)(2,1)S(1)} %bitcast.97, bf16[4096,896]{1,0:T(8,128)(2,1)} %bitcast.125), kind=kOutput, calls=%fused_computation.13 | convolution fusion | flops 1412382720 | bytes 10978048 | tf_op jit(solution)/shard_map/dot_general | solution.py:66
  265.2 32.7 %all-gather.29.cloned.1.call-done = bf16[1536,896]{1,0:T(8,128)(2,1)} async-done(((bf16[192,896]{1,0:T(8,128)(2,1)}), bf16[1536,896]{1,0:T(8,128)(2,1)}) %all-gather.29.cloned.1.call-update) | async-done | bytes 2752528 | tf_op jit(solution)/shard_map/all_gather | solution.py:23
  298.1 43.4 %all-gather.25.cloned.1.call-done = bf16[1536,896]{1,0:T(8,128)(2,1)} async-done(((bf16[192,896]{1,0:T(8,128)(2,1)}), bf16[1536,896]{1,0:T(8,128)(2,1)}) %all-gather.25.cloned.1.call-update) | async-done | bytes 2752528 | tf_op jit(solution)/shard_map/all_gather | solution.py:23
  341.7 47.2 %all_to_all.30 = bf16[16,192,256]{2,1,0:T(8,128)(2,1)S(1)} all-to-all(bf16[16,192,256]{2,1,0:T(8,128)(2,1)S(1)} %fusion.10), channel_id=1, replica_groups=mesh['z'=8,'core'=2,'mp'=16] {'z','core'}, dimensions={0} | all-to-all | bytes 3145728 | tf_op jit(solution)/shard_map/all_to_all | solution.py:48
  388.9 5.2 %convolution_convert_fusion.1 = bf16[256,896]{1,0:T(8,128)(2,1)} fusion(bf16[3072,256]{1,0:T(8,128)(2,1)S(1)} %bitcast.121, bf16[3072,896]{1,0:T(8,128)(2,1)} %bitcast.126), kind=kOutput, calls=%fused_computation.8 | convolution fusion | flops 1409515520 | bytes 7536640 | tf_op jit(solution)/shard_map/dot_general | solution.py:77
  394.1 5.2 %convolution_convert_fusion.2 = bf16[256,896]{1,0:T(8,128)(2,1)} fusion(bf16[3072,256]{1,0:T(8,128)(2,1)S(1)} %bitcast.122, bf16[3072,896]{1,0:T(8,128)(2,1)} %bitcast.127), kind=kOutput, calls=%fused_computation.9 | convolution fusion | flops 1409515520 | bytes 7536640 | tf_op jit(solution)/shard_map/dot_general | solution.py:74
  (64 shorter events, 5.9 us)
Async XLA Ops:
  7.2 56.1 %all-gather.21.cloned.1.call-start = ((), (), s32[]{:S(2)}) async-start(), calls=%async_computation.7 | async-start | bytes 4128768 | tf_op jit(solution)/shard_map/all_gather | solution.py:23
  7.9 105.6 %all-gather.17.cloned.1.call-start = ((), (), s32[]{:S(2)}) async-start(), calls=%async_computation.5 | async-start | bytes 4128768 | tf_op jit(solution)/shard_map/all_gather | solution.py:23
  8.6 244.8 %all-gather.23.cloned.1.call-start = ((), (), s32[]{:S(2)}) async-start(), calls=%async_computation.8 | async-start | bytes 11010048 | tf_op jit(solution)/shard_map/all_gather | solution.py:24
  63.3 195.2 %all-gather.19.cloned.1.call-start = ((), (), s32[]{:S(2)}) async-start(), calls=%async_computation.6 | async-start | bytes 11010048 | tf_op jit(solution)/shard_map/all_gather | solution.py:24
  113.5 0.9 copy-start.2
  116.0 6.7 %copy-start.3 = (s32[16,192]{1,0:T(8,128)S(1)}, s32[16,192]{1,0:T(8,128)}, u32[]{:S(2)}) copy-start(s32[16,192]{1,0:T(8,128)} %param.13) | copy-start | bytes 36868
  116.0 6.7 %copy-start.4 = (s32[16]{0:T(128)S(1)}, s32[16]{0:T(128)}, u32[]{:S(2)}) copy-start(s32[16]{0:T(128)} %param.14) | copy-start | bytes 196
  116.0 36.9 %all-to-all-start.3 = ((bf16[16,256,256]{1,2,0:T(8,128)(2,1)}), bf16[16,256,256]{1,2,0:T(8,128)(2,1)S(1)}, u32[]{:S(2)}, u32[]{:S(2)}) async-start(bf16[16,256,256]{1,2,0:T(8,128)(2,1)} %broadcast_in_dim.5), calls=%async_computation.3 | async-start | bytes 4194304 | tf_op jit(solution)/shard_map/all_to_all | solution.py:9
  152.9 1.3 copy-start
  154.3 47.9 %all-to-all-start = ((bf16[16,192,256]{2,1,0:T(8,128)(2,1)}), bf16[16,192,256]{2,1,0:T(8,128)(2,1)S(1)}, u32[]{:S(2)}, u32[]{:S(2)}) async-start(bf16[16,192,256]{2,1,0:T(8,128)(2,1)} %bitcast.120), calls=%async_computation | async-start | bytes 3145728 | tf_op jit(solution)/shard_map/all_to_all | solution.py:44
  160.8 4.3 %copy-start.1 = (bf16[16,256,256]{1,2,0:T(8,128)(2,1)S(1)}, bf16[16,256,256]{1,2,0:T(8,128)(2,1)}, u32[]{:S(2)}) copy-start(bf16[16,256,256]{1,2,0:T(8,128)(2,1)} %copy-done) | copy-start | bytes 6291460
  160.8 4.7 %copy-start.5 = (bf16[4096,512]{1,0:T(8,128)(2,1)S(1)}, bf16[4096,512]{1,0:T(8,128)(2,1)}, u32[]{:S(2)}) copy-start(bf16[4096,512]{1,0:T(8,128)(2,1)} %param.11) | copy-start | bytes 12582916
  160.8 4.7 %copy-start.7 = (f32[512]{0:T(512)S(1)}, f32[512]{0:T(512)}, u32[]{:S(2)}) copy-start(f32[512]{0:T(512)} %param.12) | copy-start | bytes 6148
  202.2 21.2 %all-to-all-start.4 = ((bf16[16,1,192]{2,1,0:T(2,128)(2,1)}), bf16[16,1,192]{2,1,0:T(2,128)(2,1)S(1)}, u32[]{:S(2)}, u32[]{:S(2)}) async-start(bf16[16,1,192]{2,1,0:T(2,128)(2,1)} %all_to_all.24), calls=%async_computation.4 | async-start | bytes 32768 | tf_op jit(solution)/shard_map/all_to_all | solution.py:63
  224.7 28.6 %all-to-all-start.1 = ((bf16[16,192,256]{2,1,0:T(8,128)(2,1)}), bf16[16,192,256]{2,1,0:T(8,128)(2,1)S(1)}, u32[]{:S(2)}, u32[]{:S(2)}) async-start(bf16[16,192,256]{2,1,0:T(8,128)(2,1)} %broadcast_in_dim.4), calls=%async_computation.1 | async-start | bytes 3145728 | tf_op jit(solution)/shard_map/all_to_all | solution.py:9
  228.4 69.5 %all-gather.29.cloned.1.call-start = ((), (), s32[]{:S(2)}) async-start(), calls=%async_computation.11 | async-start | bytes 3096576 | tf_op jit(solution)/shard_map/all_gather | solution.py:23
  253.5 5.0 %copy-start.6 = (bf16[192,896]{1,0:T(8,128)(2,1)S(1)}, bf16[192,896]{1,0:T(8,128)(2,1)}, u32[]{:S(2)}) copy-start(bf16[192,896]{1,0:T(8,128)(2,1)} %param.17) | copy-start | bytes 1032196
  264.5 76.9 %all-gather.25.cloned.1.call-start = ((), (), s32[]{:S(2)}) async-start(), calls=%async_computation.9 | async-start | bytes 3096576 | tf_op jit(solution)/shard_map/all_gather | solution.py:23
  265.1 123.8 %all-gather.31.cloned.1.call-start = ((), (), s32[]{:S(2)}) async-start(), calls=%async_computation.12 | async-start | bytes 8257536 | tf_op jit(solution)/shard_map/all_gather | solution.py:24
  297.9 96.2 %all-gather.27.cloned.1.call-start = ((), (), s32[]{:S(2)}) async-start(), calls=%async_computation.10 | async-start | bytes 8257536 | tf_op jit(solution)/shard_map/all_gather | solution.py:24
Sparse Core Ops, SparseCore 0:
  9.8 53.4 all-gather.20
  65.0 48.4 all-gather.16
  115.3 23.1 all-gather.22
  140.1 25.0 all-gather.18
  264.7 33.1 all-gather.28
  300.1 41.3 all-gather.24
  343.3 23.0 all-gather.30
  368.1 22.2 all-gather.26
